TPU v7x, 256 devices: a whole 4x4x8 slice. The times are simulated.
256 devices in a mesh: row: 32 (over z, x_hi, core), col: 8 (over x_lo, y).
Axes of the slice: x: 4 (x_hi: 2, x_lo: 2; x = x_hi * 2 + x_lo), y: 4, z: 8, core: 2. Of those that a mesh axis runs over, the one named last changes fastest.
Arguments:
- tokens: bfloat16 [2048, 12288], P('col', 'row'), may hold values from -6 to 6
- weight: bfloat16 [12288, 24576], P('row', 'col'), may hold values from -0.0546875 to 0.0546875
- pre_act: bfloat16 [2048, 24576], P('row', 'col'), may hold values from -6 to 6
- out_grad: bfloat16 [2048, 24576], P('row', 'col'), may hold values from -6 to 6
Outputs:
- input_grad: bfloat16 [2048, 12288], P('col', 'row')
- weight_grad: bfloat16 [12288, 24576], P('row', 'col')
- left_stats: bfloat16 [12288, 24576], P('row', 'col')
- right_stats: bfloat16 [12288, 24576], P('row', 'col')
All inputs are finite; a program needn't handle non-finite values.
Results may differ from a plain program's by a relative error of at most 0.0054.
Values may be sent and summed in bfloat16 or wider, within the bound.
A program may use at most 128 MiB of HBM per device.

v0:
```python
import math

import jax
import jax.numpy as jnp
from jax import lax
from jax.sharding import PartitionSpec as P

BLOCK = 384


def gelu_slope(value):
    coeff = math.sqrt(2.0 / math.pi)
    inner = coeff * (value + 0.044715 * value * value * value)
    tanh_u = jnp.tanh(inner)
    return 0.5 * (1.0 + tanh_u) + 0.5 * value * (1.0 - tanh_u * tanh_u) * coeff * (
        1.0 + 3.0 * 0.044715 * value * value
    )


def on_device(tokens, weight, pre_act, out_grad):
    x_all = lax.all_gather(tokens, "col", axis=0, tiled=True)
    num_tokens = x_all.shape[0]
    rows_here = weight.shape[0]
    cols_here = weight.shape[1]
    hidden_grad = (out_grad.astype(jnp.float32) * gelu_slope(pre_act.astype(jnp.float32))).astype(
        jnp.bfloat16
    )
    grad_all = lax.all_gather(hidden_grad, "row", axis=0, tiled=True)
    partial_value = lax.dot_general(
        grad_all, weight, (((1,), (1,)), ((), ())), preferred_element_type=jnp.float32
    )
    weight_sum = lax.dot_general(
        x_all, grad_all, (((0,), (0,)), ((), ())), preferred_element_type=jnp.float32
    )
    input_grad = lax.psum_scatter(partial_value, "col", scatter_dimension=0, tiled=True).astype(
        jnp.bfloat16
    )
    scale = 1.0 / (BLOCK * num_tokens)
    tiles = weight_sum.reshape(rows_here // BLOCK, BLOCK, cols_here // BLOCK, BLOCK)
    left = jnp.einsum("ipjq,irjq->ipjr", tiles, tiles, precision=lax.Precision.HIGHEST) * scale
    right = jnp.einsum("ipjq,ipjr->iqjr", tiles, tiles, precision=lax.Precision.HIGHEST) * scale
    left_stats = left.reshape(rows_here, cols_here).astype(jnp.bfloat16)
    right_stats = right.reshape(rows_here, cols_here).astype(jnp.bfloat16)
    return (input_grad, weight_sum.astype(jnp.bfloat16), left_stats, right_stats)


def solution(mesh):
    in_specs = (P("col", "row"), P("row", "col"), P("row", "col"), P("row", "col"))
    out_specs = (P("col", "row"), P("row", "col"), P("row", "col"), P("row", "col"))
    return jax.shard_map(
        on_device, mesh=mesh, in_specs=in_specs, out_specs=out_specs, check_vma=False
    )
```

profile of v0, /device:TPU:2, one launch (start us, length us, event | category | flops | bytes accessed | tf_op | source)
XLA Modules:
  0.0 232.9 jit_solution(4617175206382753291)
XLA Ops:
  7.2 0.0 copy-start
  7.2 0.0 all-gather.3.cloned.1.call-start
  7.2 2.6 %fusion.7 = bf16[64,3072]{1,0:T(8,128)(2,1)} fusion(bf16[64,3072]{1,0:T(8,128)(2,1)} %param.6, bf16[64,3072]{1,0:T(8,128)(2,1)} %param.7), kind=kLoop, calls=%fused_computation.17 | loop fusion | flops 4128768 | bytes 1179648 | tf_op jit(solution)/shard_map/convert_element_type | solution.py:25
  9.8 0.0 all-gather.3.cloned.1.call-update
  9.8 0.0 all-gather.5.cloned.1.call-start
  9.9 0.7 all-gather.5.cloned.1.call-update
  10.6 0.0 reduce-scatter.2.cloned.1.call-start
  10.6 119.9 %all-gather.3.cloned.1.call-done = bf16[2048,3072]{1,0:T(8,128)(2,1)} async-done(((bf16[64,3072]{1,0:T(8,128)(2,1)}), bf16[2048,3072]{1,0:T(8,128)(2,1)}) %all-gather.3.cloned.1.call-update) | async-done | bytes 12582928 | tf_op jit(solution)/shard_map/all_gather | solution.py:28
  130.6 0.0 copy-done
  130.6 10.8 %fusion.9 = f32[2048,384]{1,0:T(8,128)} fusion(bf16[2048,3072]{1,0:T(8,128)(2,1)} %all-gather.3.cloned.1.call-done, bf16[384,3072]{1,0:T(8,128)(2,1)S(1)} %copy-done), kind=kOutput, calls=%fused_computation.19 | convolution fusion | flops 4831838208 | bytes 18087936 | tf_op jit(solution)/shard_map/dot_general | solution.py:29
  141.4 0.0 reduce-scatter.2.cloned.1.call-update
  141.4 30.1 %all-gather.5.cloned.1.call-done = bf16[2048,384]{1,0:T(8,128)(2,1)} async-done(((bf16[256,384]{1,0:T(8,128)(2,1)}), bf16[2048,384]{1,0:T(8,128)(2,1)}) %all-gather.5.cloned.1.call-update) | async-done | bytes 1572880 | tf_op jit(solution)/shard_map/all_gather | solution.py:21
  171.5 12.1 %bitcast_convert_fusion = (bf16[384,3072]{0,1:T(8,128)(2,1)}, f32[3072,384]{1,0:T(8,128)}) fusion(bf16[2048,3072]{1,0:T(8,128)(2,1)} %all-gather.3.cloned.1.call-done, bf16[2048,384]{1,0:T(8,128)(2,1)} %all-gather.5.cloned.1.call-done), kind=kOutput, calls=%fused_computation | convolution fusion | flops 4833017856 | bytes 21233664 | tf_op jit(solution)/shard_map/dot_general | solution.py:32
  183.6 4.3 %copy.11 = bf16[384,3072]{1,0:T(8,128)(2,1)} copy(bf16[384,3072]{0,1:T(8,128)(2,1)} %get-tuple-element.8) | data formatting | bytes 4718592
  187.9 14.0 %multiply_convert_fusion.1 = bf16[8,384,384]{2,1,0:T(8,128)(2,1)} fusion(f32[384,8,384]{0,2,1:T(8,128)} %bitcast.22), kind=kOutput, calls=%fused_computation.2 | convolution fusion | flops 5438177280 | bytes 7077888 | tf_op jit(solution)/shard_map/ipjq,irjq->ipjr/dot_general | solution.py:40
  201.9 4.3 %copy.12 = bf16[384,3072]{1,0:T(8,128)(2,1)} copy(bf16[384,3072]{0,1:T(8,128)(2,1)} %bitcast.25) | data formatting | bytes 4718592
  206.2 14.2 %multiply_convert_fusion = bf16[8,384,384]{2,1,0:T(8,128)(2,1)} fusion(f32[384,8,384]{0,2,1:T(8,128)} %bitcast.23), kind=kOutput, calls=%fused_computation.1 | convolution fusion | flops 5438177280 | bytes 7077888 | tf_op jit(solution)/shard_map/ipjq,ipjr->iqjr/dot_general | solution.py:41
  220.4 4.3 %copy.13 = bf16[384,3072]{1,0:T(8,128)(2,1)} copy(bf16[384,3072]{0,1:T(8,128)(2,1)} %bitcast.24) | data formatting | bytes 4718592
  224.7 0.0 reduce-scatter.2.cloned.1.call-done
  224.7 1.7 convert_element_type.42
Async XLA Ops:
  7.2 123.4 %copy-start = (bf16[384,3072]{1,0:T(8,128)(2,1)S(1)}, bf16[384,3072]{1,0:T(8,128)(2,1)}, u32[]{:S(2)}) copy-start(bf16[384,3072]{1,0:T(8,128)(2,1)} %param.5) | copy-start | bytes 7077892
  7.2 123.4 %all-gather.3.cloned.1.call-start = ((), (), s32[]{:S(2)}) async-start(), calls=%async_computation.1 | async-start | bytes 12976128 | tf_op jit(solution)/shard_map/all_gather | solution.py:28
  9.8 161.7 %all-gather.5.cloned.1.call-start = ((), (), s32[]{:S(2)}) async-start(), calls=%async_computation.3 | async-start | bytes 1769472 | tf_op jit(solution)/shard_map/all_gather | solution.py:21
  10.6 214.1 %reduce-scatter.2.cloned.1.call-start = ((), (), s32[]{:S(2)}) async-start(), calls=%async_computation.2 | async-start | bytes 3538944 | tf_op jit(solution)/shard_map/reduce_scatter | solution.py:35
Sparse Core Ops, SparseCore 0:
  11.3 119.1 all-gather.2
  132.3 39.1 all-gather.4
  174.1 48.9 reduce-scatter.1
where the time goes:
time: 234 us; the launch traced here: 233 us
  waiting for transfers between devices  151 us (65%)
  matrix products  51.1 us (22%)
  between operations  13.8 us (6%)
  local copies, waits for them, and re-layouts  12.9 us (6%)
  other arithmetic  4.26 us (2%)
    all_gather x1, waiting for transfers between devices, on_device(): grad_all = lax.all_gather(hidden_grad, 'row', axis=0, tiled=True)  120 us
    all_gather x1, waiting for transfers between devices, on_device(): x_all = lax.all_gather(tokens, 'col', axis=0, tiled=True)  30.1 us
    dot_general x1, matrix products, on_device(): jnp.einsum('ipjq,ipjr->iqjr', tiles, tiles, precision=lax.Precision.HIGHEST)  14.2 us
    dot_general x1, matrix products, on_device(): jnp.einsum('ipjq,irjq->ipjr', tiles, tiles, precision=lax.Precision.HIGHEST)  14 us
    unnamed x5, local copies, waits for them, and re-layouts  12.9 us
    dot_general x1, matrix products, on_device(): lax.dot_general(x_all, grad_all, (((0,), (0,)), ((), ())), preferred_elem...  12.1 us
    dot_general x1, matrix products, on_device(): lax.dot_general(grad_all, weight, (((1,), (1,)), ((), ())), preferred_ele...  10.8 us
  transfers between devices with their start and end apart: 3, of which 2 were waited for; matrix products, arithmetic and copies ran while one was open for 27% of the time, Pallas kernels for 0%

commit v1 on v0

v1 whole, which is shorter than its diff:
```python
import functools
import math

import jax
import jax.numpy as jnp
from jax import lax
from jax.experimental import pallas as pl
from jax.experimental.pallas import tpu as pltpu
from jax.sharding import PartitionSpec as P

MESH = pl.DeviceIdType.MESH
BF, F32 = jnp.bfloat16, jnp.float32
BLOCK = 384
LATE = 2
NT = (((1,), (1,)), ((), ()))
NN = (((1,), (0,)), ((), ()))
DIST = (0, 1, 7, 2, 6, 3, 5, 4)
GROUPS = ((0, 768, False), (768, 768, True), (1536, 768, False), (2304, 768, True))
PHASES = ((0, 1), (2, 3))
HALF = 1536


def gelu_slope(value):
    coeff = math.sqrt(2.0 / math.pi)
    inner = coeff * (value + 0.044715 * value * value * value)
    tanh_u = jnp.tanh(inner)
    return 0.5 * (1.0 + tanh_u) + 0.5 * value * (1.0 - tanh_u * tanh_u) * coeff * (
        1.0 + 3.0 * 0.044715 * value * value
    )


def mm(a, b, dims=NN):
    return lax.dot_general(a, b, dims, preferred_element_type=F32)


def statistics(g, scale):
    hi = g.astype(BF)
    lo = (g - hi.astype(F32)).astype(BF)
    hi_t, lo_t = hi.T, lo.T
    a = mm(hi, lo_t)
    left = mm(hi, hi_t) + (a + a.T)
    b = mm(hi_t, lo)
    right = mm(hi_t, hi) + (b + b.T)
    return hi, (left * scale).astype(BF), (right * scale).astype(BF)


def slot_of(d):
    far = d // 5
    return (1 - far) * (2 * d - 1) + far * (16 - 2 * d) + (7 - d) // 7


def kernel(scale, early, tok_in, wt_in, pre_in, og_in, done_out, rest_out, dx_out,
           hid, wt, pre, og, tok_raw, tok_own, tok, dxacc, dxs, dxr, xs, xr, dxo, dw, outs,
           lsem, rsem, bsem, tsem, dsem, xsem, zs_sem, xs_sem, bs_sem, ts_sem, ds_sem, os_sem):
    r = lax.axis_index("row")
    c = lax.axis_index("col")
    core = r % 2
    xh = (r // 2) % 2
    z = r // 4
    xl = c // 4
    y = c % 4

    def row_id(zz, hh, cc):
        return (zz * 2 + hh) * 2 + cc

    sib = (row_id(z, xh, 1 - core), c)
    up = (row_id((z + 1) % 8, xh, core), c)
    down = (row_id((z + 7) % 8, xh, core), c)
    last = (row_id((z + 1 + 6 * core) % 8, xh, core), c)
    across = (row_id(z, 1 - xh, core), c)
    xpeer = (r, (1 - xl) * 4 + y)
    ypeer = [None] + [(r, xl * 4 + (y + j) % 4) for j in (1, 2, 3)]

    bar = pltpu.get_barrier_semaphore()
    peers = [sib, up, down, across, xpeer] + ypeer[1:]
    for peer in peers:
        pl.semaphore_signal(bar, inc=1, device_id=peer, device_id_type=MESH)

    loads = [
        pltpu.make_async_copy(pre_in, pre, lsem.at[0]),
        pltpu.make_async_copy(og_in, og, lsem.at[1]),
        pltpu.make_async_copy(tok_in, tok_raw, lsem.at[2]),
        pltpu.make_async_copy(wt_in, wt, lsem.at[3]),
    ]
    for cp in loads:
        cp.start()

    rows_of = [pl.multiple_of((xh * 2 + core) * 64, 64), pl.multiple_of(((1 - xh) * 2 + core) * 64, 64)]
    sib_rows = [pl.multiple_of((xh * 2 + 1 - core) * 64, 64), pl.multiple_of(((1 - xh) * 2 + 1 - core) * 64, 64)]

    def piece(g, slot, rows):
        return hid.at[slot, pl.ds(rows, 64), pl.ds(GROUPS[g][0], GROUPS[g][1])]

    sent = []

    def push(src, dst, send_sem, recv_sem, to):
        cp = pltpu.make_async_remote_copy(src_ref=src, dst_ref=dst, send_sem=send_sem, recv_sem=recv_sem,
                                          device_id=to, device_id_type=MESH)
        cp.start()
        sent.append(cp)

    def arrived(dst, recv_sem, frm):
        pltpu.make_async_remote_copy(src_ref=dst, dst_ref=dst, send_sem=lsem.at[7], recv_sem=recv_sem,
                                     device_id=frm, device_id_type=MESH).wait_recv()

    def push_z(g, p, src, dst, to):
        push(piece(g, src, rows_of[p]), piece(g, dst, rows_of[p]), zs_sem.at[g, p, dst], rsem.at[g, p, dst], to)

    def forward(g, p, slot):
        once = GROUPS[g][2]
        if p == 0 and once and slot == 0:
            push(piece(g, 0, rows_of[0]), piece(g, 0, rows_of[0]), xs_sem.at[g, 0], rsem.at[g, 1, 0], across)
        if p == 0 or once:
            if slot in (0, 1, 3):
                push_z(g, p, slot, slot + 2 if slot else 1, down)
            if slot in (0, 2, 4):
                push_z(g, p, slot, slot + 2, up)
        if p == 0 and not once:
            push(piece(g, slot, rows_of[0]), piece(g, slot, rows_of[0]), xs_sem.at[g, slot], rsem.at[g, 1, slot],
                 across)
        push(piece(g, slot, rows_of[p]), piece(g, slot, rows_of[p]), bs_sem.at[g, p, slot], bsem.at[g, p, slot], sib)

    def got(g, p, slots):
        frm = across if p == 1 else up
        for slot in slots:
            arrived(piece(g, slot, rows_of[p]), rsem.at[g, p, slot], frm)
            forward(g, p, slot)
        if 5 in slots and (p == 0 or GROUPS[g][2]):
            push_z(g, p, 6 - core, 7, last)

    def sibling(phase, slots):
        for slot in slots:
            for g in PHASES[phase]:
                for p in (0, 1):
                    arrived(piece(g, slot, sib_rows[p]), bsem.at[g, p, slot], sib)

    def hidden(phase):
        for k in range(4):
            cols = pl.ds(phase * HALF + k * BLOCK, BLOCK)
            val = og[:, cols].astype(F32) * gelu_slope(pre[:, cols].astype(F32))
            hid[0, pl.ds(rows_of[0], 64), cols] = val.astype(BF)

    def dx_task(phase, first, n):
        cols = pl.ds(phase * HALF, HALF)
        val = mm(hid[pl.ds(first, n), :, cols].reshape(n * 256, HALF), wt[:, cols], NT)
        val = val.reshape(n, 256, BLOCK)
        if phase == 0:
            dxacc[pl.ds(first, n)] = val
        else:
            val = val + dxacc[pl.ds(first, n)]
            dxacc[pl.ds(first, n)] = val
            dxs[pl.ds(first, n)] = val.astype(BF)

    def dx_send(slots):
        for slot in slots:
            t = (z + DIST[slot]) % 8
            to_x, to_y = t // 4, t % 4
            j = (to_y + 4 - y) % 4

            @pl.when(j != 0)
            def _():
                pltpu.make_async_remote_copy(
                    src_ref=dxs.at[slot], dst_ref=dxr.at[to_x, j], send_sem=ds_sem.at[slot],
                    recv_sem=dsem.at[to_x, j], device_id=(r, xl * 4 + to_y), device_id_type=MESH).start()

    def dw_all(phase, k):
        cols = pl.ds(phase * HALF + k * 768, 768)
        dw[:, cols] = mm(tok[...], hid[:, :, cols].reshape(2048, 768))

    def dw_part(first, n, fresh):
        for k in range(2):
            cols = pl.ds(HALF + k * 768, 768)
            val = mm(tok[:, pl.ds(first * 256, n * 256)], hid[pl.ds(first, n), :, cols].reshape(n * 256, 768))
            dw[:, cols] = val if fresh else dw[:, cols] + val

    pending = []
    written = []

    def flush():
        for b in pending:
            cp = pltpu.make_async_copy(outs.at[:, :, pl.ds(b * BLOCK, BLOCK)],
                                       done_out.at[:, :, pl.ds(b * BLOCK, BLOCK)], os_sem.at[b])
            cp.start()
            written.append(cp)
        pending.clear()

    def stats(b):
        flush()
        cols = pl.ds(b * BLOCK, BLOCK)
        grad, left, right = statistics(dw[:, cols], scale)
        outs[0, :, cols] = grad
        outs[1, :, cols] = left
        outs[2, :, cols] = right
        pending.append(b)

    loads[0].wait()
    loads[1].wait()
    hidden(0)
    loads[2].wait()
    tok_own[...] = tok_raw[...].T
    pl.semaphore_wait(bar, len(peers))

    def own(phase):
        g_every, g_once = PHASES[phase]
        push(piece(g_once, 0, rows_of[0]), piece(g_once, 0, rows_of[0]), xs_sem.at[g_once, 0], rsem.at[g_once, 1, 0],
             across)
        for g in PHASES[phase]:
            push_z(g, 0, 0, 1, down)
            push_z(g, 0, 0, 2, up)
        push(piece(g_every, 0, rows_of[0]), piece(g_every, 0, rows_of[0]), xs_sem.at[g_every, 0],
             rsem.at[g_every, 1, 0], across)
        for g in PHASES[phase]:
            push(piece(g, 0, rows_of[0]), piece(g, 0, rows_of[0]), bs_sem.at[g, 0, 0], bsem.at[g, 0, 0], sib)

    own(0)

    def tok_at(col):
        return tok.at[:, pl.ds(pl.multiple_of(slot_of((col + 8 - z) % 8) * 256, 256), 256)]

    push(tok_own, tok_at(c), ts_sem.at[0, 0], tsem.at[0, 0], xpeer)
    for j in (1, 2, 3):
        push(tok_own, tok_at(c), ts_sem.at[0, j], tsem.at[0, j], ypeer[j])
    keep = pltpu.make_async_copy(tok_own, tok_at(c), lsem.at[4])
    keep.start()
    hidden(1)
    loads[3].wait()

    def tok_relay():
        other = (1 - xl) * 4 + y
        arrived(tok_at(other), tsem.at[0, 0], xpeer)
        for j in (1, 2, 3):
            push(tok_at(other), tok_at(other), ts_sem.at[1, j], tsem.at[1, j], ypeer[j])

    def tok_wait():
        keep.wait()
        for j in (1, 2, 3):
            src_y = (y + 4 - j) % 4
            arrived(tok_at(xl * 4 + src_y), tsem.at[0, j], ypeer[j])
            arrived(tok_at((1 - xl) * 4 + src_y), tsem.at[1, j], ypeer[j])

    fill = [lambda: (tok_wait(), dw_all(0, 0)), lambda: dw_all(0, 1)] + [functools.partial(stats, b) for b in range(4)]

    def filler(phase, n=1):
        if phase:
            for _ in range(n):
                if fill:
                    fill.pop(0)()

    def near(phase, s):
        first, n = (0, 1) if s == 0 else (7, 1) if s == 4 else (2 * s - 1, 2)
        sibling(phase, range(first, first + n))
        dx_task(phase, first, n)
        return first, n

    for phase in (0, 1):
        every, once = PHASES[phase]
        for s in (1, 2, 3, 4):
            now = (7,) if s == 4 else (2 * s - 1, 2 * s)
            before = (0,) if s == 1 else (2 * s - 3, 2 * s - 2)
            if s == 4 and phase == 0:
                own(1)
            got(every, 0, now)
            filler(phase)
            got(once, 1, before)
            filler(phase)
            got(once, 0, now)
            got(every, 1, before)
            if phase == 0 and s == 1:
                tok_relay()
            first, n = near(phase, s - 1)
            if phase:
                dw_part(first, n, s == 1)
                dx_send(range(first, first + n))
        got(once, 1, (7,))
        filler(phase)
        got(every, 1, (7,))
        near(phase, 4)
        if phase:
            filler(phase, 9)
            dx_send((7,))
            dw_part(7, 1, False)

    rest = pltpu.make_async_copy(dw.at[:, pl.ds(early * BLOCK, (8 - early) * BLOCK)], rest_out, lsem.at[5])
    for b in range(4, early):
        stats(b)
    rest.start()

    def total(at_x):
        t = at_x * 4 + y
        val = dxacc[slot_of((t + 8 - z) % 8)]
        for j in (1, 2, 3):
            arrived(dxr.at[at_x, j], dsem.at[at_x, j], ypeer[j])
            val = val + dxr[at_x, j].astype(F32)
        return val

    xs[...] = total(1 - xl).astype(BF)
    flush()
    dxo_mine = total(xl)
    push(xs, xr, xsem.at[0], xsem.at[1], xpeer)
    arrived(xr, xsem.at[1], xpeer)
    dxo[...] = (dxo_mine + xr[...].astype(F32)).astype(BF)
    out = pltpu.make_async_copy(dxo, dx_out, lsem.at[6])
    out.start()
    for cp in sent:
        cp.wait_send()
    for slot in range(8):
        t = (z + DIST[slot]) % 8

        @pl.when((t % 4 + 4 - y) % 4 != 0)
        def _():
            pltpu.make_async_remote_copy(
                src_ref=dxs.at[slot], dst_ref=dxr.at[0, 1], send_sem=ds_sem.at[slot],
                recv_sem=dsem.at[0, 1], device_id=xpeer, device_id_type=MESH).wait_send()

    for cp in written:
        cp.wait()
    rest.wait()
    out.wait()


def finish(scale, early, done_in, rest_in, dx_in, gw_out, left_out, right_out, dx_out,
           done, rest, outs, dxv, isem, osem, rsem):
    late = 8 - early
    cps = [pltpu.make_async_copy(rest_in, rest, rsem), pltpu.make_async_copy(dx_in, dxv, isem.at[3])]
    cps += [pltpu.make_async_copy(done_in.at[i], done.at[i], isem.at[i]) for i in range(3)]
    for cp in cps:
        cp.start()
    hbm = (gw_out, left_out, right_out)
    res = []

    def put(src, dst, sem):
        cp = pltpu.make_async_copy(src, dst, sem)
        cp.start()
        res.append(cp)

    cps[0].wait()
    for k in range(late):
        cols = pl.ds(k * BLOCK, BLOCK)
        vals = statistics(rest[:, cols], scale)
        for i in range(3):
            outs[i, :, cols] = vals[i]
        if k == 0:
            for i in range(3):
                cps[2 + i].wait()
                put(done.at[i], hbm[i].at[:, pl.ds(0, early * BLOCK)], osem.at[8, i])
        for i in range(3):
            put(outs.at[i, :, cols], hbm[i].at[:, pl.ds((early + k) * BLOCK, BLOCK)], osem.at[k, i])
    cps[1].wait()
    put(dxv, dx_out, isem.at[4])
    for cp in res:
        cp.wait()


def on_device(tokens, weight, pre_act, out_grad):
    early = 8 - LATE
    scale = 1.0 / (BLOCK * 2048)
    anyspec = pl.BlockSpec(memory_space=pl.ANY)
    dma, vmem = pltpu.SemaphoreType.DMA, pltpu.VMEM
    done, rest, dx = pl.pallas_call(
        functools.partial(kernel, scale, early),
        out_shape=(
            jax.ShapeDtypeStruct((3, BLOCK, early * BLOCK), BF),
            jax.ShapeDtypeStruct((BLOCK, LATE * BLOCK), F32),
            jax.ShapeDtypeStruct((256, BLOCK), BF),
        ),
        in_specs=[anyspec] * 4,
        out_specs=(anyspec,) * 3,
        scratch_shapes=[
            vmem((8, 256, 3072), BF), vmem((BLOCK, 3072), BF), vmem((64, 3072), BF), vmem((64, 3072), BF),
            vmem((256, BLOCK), BF), vmem((BLOCK, 256), BF), vmem((BLOCK, 2048), BF),
            vmem((8, 256, BLOCK), F32), vmem((8, 256, BLOCK), BF), vmem((2, 4, 256, BLOCK), BF),
            vmem((256, BLOCK), BF), vmem((256, BLOCK), BF), vmem((256, BLOCK), BF),
            vmem((BLOCK, 3072), F32), vmem((3, BLOCK, early * BLOCK), BF),
            dma((8,)), dma((4, 2, 8)), dma((4, 2, 8)), dma((2, 4)), dma((2, 4)), dma((2,)),
            dma((4, 2, 8)), dma((4, 8)), dma((4, 2, 8)), dma((2, 4)), dma((8,)), dma((8,)),
        ],
        compiler_params=pltpu.CompilerParams(collective_id=0, has_side_effects=True,
                                             vmem_limit_bytes=60 * 2**20),
        name="exchange",
    )(tokens, weight, pre_act, out_grad)
    full = jax.ShapeDtypeStruct((BLOCK, 3072), BF)
    gw, left, right, dx = pl.pallas_call(
        functools.partial(finish, scale, early),
        out_shape=(full, full, full, jax.ShapeDtypeStruct((256, BLOCK), BF)),
        in_specs=[anyspec] * 3,
        out_specs=(anyspec,) * 4,
        scratch_shapes=[
            vmem((3, BLOCK, early * BLOCK), BF), vmem((BLOCK, LATE * BLOCK), F32), vmem((3, BLOCK, LATE * BLOCK), BF),
            vmem((256, BLOCK), BF), dma((5,)), dma((9, 3)), dma,
        ],
        compiler_params=pltpu.CompilerParams(vmem_limit_bytes=32 * 2**20),
        name="finish",
    )(done, rest, dx)
    return dx, gw, left, right


def solution(mesh):
    specs = (P("col", "row"), P("row", "col"), P("row", "col"), P("row", "col"))
    return jax.shard_map(on_device, mesh=mesh, in_specs=specs, out_specs=specs, check_vma=False)
```

time: 234 us -> 98.2 us (0.42)
  waiting for transfers between devices: 151 us -> 0 us
  Pallas kernels: 0 us -> 92.3 us
  matrix products: 51.1 us -> 0 us
  between operations: 13.8 us -> 0.81 us
  local copies, waits for them, and re-layouts: 12.9 us -> 4.69 us
  other arithmetic: 4.26 us -> 0 us
    all_gather x2 -> x0, waiting for transfers between devices: 150 us -> none  [the longest x1 120 us: on_device(): grad_all = lax.all_gather(hidden_grad, 'row', axis=0, tiled=True)]
    pallas_call x0 -> x2, Pallas kernels: none -> 92.3 us  [the longest x1 86.6 us: on_device(): pl.pallas_call(functools.partial(kernel, scale, early), out_shape=(jax.Sh...]
    dot_general x4 -> x0, matrix products: 51.1 us -> none  [the longest x1 14.2 us: on_device(): jnp.einsum('ipjq,ipjr->iqjr', tiles, tiles, precision=lax.Precision.HIGHEST)]
    unnamed x5 -> x6, local copies, waits for them, and re-layouts: 12.9 us -> 4.69 us
    convert_element_type x2 -> x0, other arithmetic: 4.26 us -> none  [the longest x1 2.56 us: on_device(): (out_grad.astype(jnp.float32) * gelu_slope(pre_act.astype(jnp.float32)))....]
  transfers between devices with their start and end apart: 3 -> 0, of which waited for: 2 -> 0; matrix products, arithmetic and copies ran while one was open for 27% -> 0% of each run, Pallas kernels for 0% -> 0%
where the time goes in v1:
time: 98.2 us; the launch traced here: 97.8 us
  Pallas kernels  92.3 us (94%)
  local copies, waits for them, and re-layouts  4.69 us (5%)
    pallas_call x1, Pallas kernels, on_device(): pl.pallas_call(functools.partial(kernel, scale, early), out_shape=(jax.Sh...  86.6 us
    pallas_call x1, Pallas kernels, on_device(): pl.pallas_call(functools.partial(finish, scale, early), out_shape=(full,...  5.74 us
    unnamed x6, local copies, waits for them, and re-layouts  4.69 us

profile of v1, /device:TPU:2, one launch (start us, length us, event | category | flops | bytes accessed | tf_op | source)
XLA Modules:
  0.0 97.8 jit_solution(15969524350653479936)
XLA Ops:
  0.6 86.6 %exchange.1 = (bf16[3,384,2304]{2,1,0:T(8,128)(2,1)}, f32[384,768]{1,0:T(8,128)}, bf16[256,384]{1,0:T(8,128)(2,1)}) custom-call(bf16[256,384]{1,0:T(8,128)(2,1)} %tok_in.1, bf16[384,3072]{1,0:T(8,128)(2,1)} %wt_in.1, bf16[64,3072]{1,0:T(8,128)(2,1)} %pre_in.1, bf16[64,3072]{1,0:T(8,128)(2,1)} %og_in.1), custom_call_target="tpu_custom_call" | custom-call | tf_op jit(solution)/shard_map/exchange/pallas_call | solution.py:359
  87.2 0.0 copy-start
  87.3 2.5 %copy-done = bf16[3,384,2304]{2,1,0:T(8,128)(2,1)S(1)} copy-done((bf16[3,384,2304]{2,1,0:T(8,128)(2,1)S(1)}, bf16[3,384,2304]{2,1,0:T(8,128)(2,1)}, u32[]{:S(2)}) %copy-start) | copy-done | bytes 5308440
  89.7 0.0 copy-start.1
  89.8 1.3 %copy-done.1 = f32[384,768]{1,0:T(8,128)S(1)} copy-done((f32[384,768]{1,0:T(8,128)S(1)}, f32[384,768]{1,0:T(8,128)}, u32[]{:S(2)}) %copy-start.1) | copy-done | bytes 1179672
  91.0 0.0 copy-start.2
  91.0 0.9 copy-done.2
  91.9 5.7 %finish.1 = (bf16[384,3072]{1,0:T(8,128)(2,1)}, bf16[384,3072]{1,0:T(8,128)(2,1)}, bf16[384,3072]{1,0:T(8,128)(2,1)}, bf16[256,384]{1,0:T(8,128)(2,1)}) custom-call(bf16[3,384,2304]{2,1,0:T(8,128)(2,1)S(1)} %copy-done, f32[384,768]{1,0:T(8,128)S(1)} %copy-done.1, bf16[256,384]{1,0:T(8,128)(2,1)S(1)} %copy-done.2), custom_call_target="tpu_custom_call" | custom-call | tf_op jit(solution)/shard_map/finish/pallas_call | solution.py:382
Async XLA Ops:
  87.2 2.5 %copy-start = (bf16[3,384,2304]{2,1,0:T(8,128)(2,1)S(1)}, bf16[3,384,2304]{2,1,0:T(8,128)(2,1)}, u32[]{:S(2)}) copy-start(bf16[3,384,2304]{2,1,0:T(8,128)(2,1)} %get-tuple-element.11.done_in) | copy-start | bytes 15925252
  89.7 1.3 %copy-start.1 = (f32[384,768]{1,0:T(8,128)S(1)}, f32[384,768]{1,0:T(8,128)}, u32[]{:S(2)}) copy-start(f32[384,768]{1,0:T(8,128)} %get-tuple-element.12.rest_in) | copy-start | bytes 3538948
  91.0 0.9 copy-start.2

commit v2 on v1

--- a/solution.py
+++ b/solution.py
@@ -15,8 +15,18 @@
 NT = (((1,), (1,)), ((), ()))
 NN = (((1,), (0,)), ((), ()))
 DIST = (0, 1, 7, 2, 6, 3, 5, 4)
-GROUPS = ((0, 768, False), (768, 768, True), (1536, 768, False), (2304, 768, True))
-PHASES = ((0, 1), (2, 3))
+W = 768
+NB = 3072 // W
+NONCE = (NB // 4, NB // 4)
+GROUPS = tuple((g * W, W, g % (NB // 2) >= NB // 2 - NONCE[g // (NB // 2)]) for g in range(NB))
+PHASES = (tuple(range(NB // 2)), tuple(range(NB // 2, NB)))
+ONCE = tuple(tuple(g for g in ph if GROUPS[g][2]) for ph in PHASES)
+EVERY = tuple(tuple(g for g in ph if not GROUPS[g][2]) for ph in PHASES)
+LEVEL = ((0,), (1, 2), (3, 4), (5, 6), (7,))
+LAG = 1
+LAG2 = 1
+OWN2 = 4
+FILL_N = 2
 HALF = 1536
 
 
@@ -201,14 +211,16 @@
     pl.semaphore_wait(bar, len(peers))
 
     def own(phase):
-        g_every, g_once = PHASES[phase]
-        push(piece(g_once, 0, rows_of[0]), piece(g_once, 0, rows_of[0]), xs_sem.at[g_once, 0], rsem.at[g_once, 1, 0],
-             across)
-        for g in PHASES[phase]:
+        def over_x(g):
+            push(piece(g, 0, rows_of[0]), piece(g, 0, rows_of[0]), xs_sem.at[g, 0], rsem.at[g, 1, 0], across)
+
+        for g in ONCE[phase]:
+            over_x(g)
+        for g in EVERY[phase] + ONCE[phase]:
             push_z(g, 0, 0, 1, down)
             push_z(g, 0, 0, 2, up)
-        push(piece(g_every, 0, rows_of[0]), piece(g_every, 0, rows_of[0]), xs_sem.at[g_every, 0],
-             rsem.at[g_every, 1, 0], across)
+        for g in EVERY[phase]:
+            over_x(g)
         for g in PHASES[phase]:
             push(piece(g, 0, rows_of[0]), piece(g, 0, rows_of[0]), bs_sem.at[g, 0, 0], bsem.at[g, 0, 0], sib)
 
@@ -238,47 +250,58 @@
             arrived(tok_at(xl * 4 + src_y), tsem.at[0, j], ypeer[j])
             arrived(tok_at((1 - xl) * 4 + src_y), tsem.at[1, j], ypeer[j])
 
-    fill = [lambda: (tok_wait(), dw_all(0, 0)), lambda: dw_all(0, 1)] + [functools.partial(stats, b) for b in range(4)]
-
-    def filler(phase, n=1):
+    fill = [lambda: dw_all(0, 0), lambda: dw_all(0, 1)] + [functools.partial(stats, b) for b in range(4)]
+
+    def filler(n=1):
+        for _ in range(n):
+            if fill:
+                fill.pop(0)()
+
+    def near(phase, s):
+        first, n = LEVEL[s][0], len(LEVEL[s])
+        sibling(phase, LEVEL[s])
+        dx_task(phase, first, n)
+        if (phase, s) == (0, 4):
+            tok_wait()
         if phase:
-            for _ in range(n):
-                if fill:
-                    fill.pop(0)()
-
-    def near(phase, s):
-        first, n = (0, 1) if s == 0 else (7, 1) if s == 4 else (2 * s - 1, 2)
-        sibling(phase, range(first, first + n))
-        dx_task(phase, first, n)
-        return first, n
-
-    for phase in (0, 1):
-        every, once = PHASES[phase]
-        for s in (1, 2, 3, 4):
-            now = (7,) if s == 4 else (2 * s - 1, 2 * s)
-            before = (0,) if s == 1 else (2 * s - 3, 2 * s - 2)
-            if s == 4 and phase == 0:
+            dw_part(first, n, s == 0)
+            dx_send(LEVEL[s])
+
+    def lazy(phase, s):
+        if s == 4:
+            for g in ONCE[phase]:
+                got(g, 1, LEVEL[4])
+        for g in EVERY[phase]:
+            got(g, 1, LEVEL[s])
+
+    order = [(phase, s) for phase in (0, 1) for s in range(5)]
+    lazies, nears = list(order), list(order)
+
+    def at(step):
+        return step[0] * 4 + step[1]
+
+    for step in order + [(1, s) for s in range(5, 5 + LAG + LAG2)]:
+        phase, s = step
+        if 1 <= s <= 4:
+            if at(step) == OWN2:
                 own(1)
-            got(every, 0, now)
-            filler(phase)
-            got(once, 1, before)
-            filler(phase)
-            got(once, 0, now)
-            got(every, 1, before)
-            if phase == 0 and s == 1:
-                tok_relay()
-            first, n = near(phase, s - 1)
-            if phase:
-                dw_part(first, n, s == 1)
-                dx_send(range(first, first + n))
-        got(once, 1, (7,))
-        filler(phase)
-        got(every, 1, (7,))
-        near(phase, 4)
-        if phase:
-            filler(phase, 9)
-            dx_send((7,))
-            dw_part(7, 1, False)
+            for g in EVERY[phase]:
+                got(g, 0, LEVEL[s])
+            for g in ONCE[phase]:
+                got(g, 1, LEVEL[s - 1])
+            for g in ONCE[phase]:
+                got(g, 0, LEVEL[s])
+        if s == 0:
+            continue
+        if at(step) == 2:
+            tok_relay()
+        while lazies and (at(lazies[0]) + LAG <= at(step)) and lazies[0][0] * 5 + lazies[0][1] <= phase * 5 + s:
+            lazy(*lazies.pop(0))
+        while nears and at(nears[0]) + LAG + LAG2 <= at(step) and (not lazies or nears[0] < lazies[0]):
+            near(*nears.pop(0))
+        if (0, 4) not in nears and s <= 4:
+            filler(FILL_N)
+    filler(9)
 
     rest = pltpu.make_async_copy(dw.at[:, pl.ds(early * BLOCK, (8 - early) * BLOCK)], rest_out, lsem.at[5])
     for b in range(4, early):
@@ -371,8 +394,8 @@
             vmem((8, 256, BLOCK), F32), vmem((8, 256, BLOCK), BF), vmem((2, 4, 256, BLOCK), BF),
             vmem((256, BLOCK), BF), vmem((256, BLOCK), BF), vmem((256, BLOCK), BF),
             vmem((BLOCK, 3072), F32), vmem((3, BLOCK, early * BLOCK), BF),
-            dma((8,)), dma((4, 2, 8)), dma((4, 2, 8)), dma((2, 4)), dma((2, 4)), dma((2,)),
-            dma((4, 2, 8)), dma((4, 8)), dma((4, 2, 8)), dma((2, 4)), dma((8,)), dma((8,)),
+            dma((8,)), dma((NB, 2, 8)), dma((NB, 2, 8)), dma((2, 4)), dma((2, 4)), dma((2,)),
+            dma((NB, 2, 8)), dma((NB, 8)), dma((NB, 2, 8)), dma((2, 4)), dma((8,)), dma((8,)),
         ],
         compiler_params=pltpu.CompilerParams(collective_id=0, has_side_effects=True,
                                              vmem_limit_bytes=60 * 2**20),
@@ -388,7 +411,7 @@
             vmem((3, BLOCK, early * BLOCK), BF), vmem((BLOCK, LATE * BLOCK), F32), vmem((3, BLOCK, LATE * BLOCK), BF),
             vmem((256, BLOCK), BF), dma((5,)), dma((9, 3)), dma,
         ],
-        compiler_params=pltpu.CompilerParams(vmem_limit_bytes=32 * 2**20),
+        compiler_params=pltpu.CompilerParams(vmem_limit_bytes=60 * 2**20),
         name="finish",
     )(done, rest, dx)
     return dx, gw, left, right

time: 98.2 us -> 89.5 us (0.911)
  local copies, waits for them, and re-layouts: 4.69 us -> 0 us
  Pallas kernels: 92.3 us -> 88.6 us
    unnamed x6 -> x0, local copies, waits for them, and re-layouts: 4.69 us -> none
    pallas_call x1, Pallas kernels: 86.6 us -> 82 us  [on_device(): pl.pallas_call(functools.partial(kernel, scale, early), out_shape=(jax.Sh...]
where the time goes in v2:
time: 89.5 us; the launch traced here: 89.4 us
  Pallas kernels  88.6 us (99%)
    pallas_call x1, Pallas kernels, on_device(): pl.pallas_call(functools.partial(kernel, scale, early), out_shape=(jax.Sh...  82 us
    pallas_call x1, Pallas kernels, on_device(): pl.pallas_call(functools.partial(finish, scale, early), out_shape=(full,...  6.62 us

profile of v2, /device:TPU:2, one launch (start us, length us, event | category | flops | bytes accessed | tf_op | source)
XLA Modules:
  0.0 89.4 jit_solution(900486049601013335)
XLA Ops:
  0.6 82.0 %exchange.1 = (bf16[3,384,2304]{2,1,0:T(8,128)(2,1)}, f32[384,768]{1,0:T(8,128)}, bf16[256,384]{1,0:T(8,128)(2,1)}) custom-call(bf16[256,384]{1,0:T(8,128)(2,1)} %tok_in.1, bf16[384,3072]{1,0:T(8,128)(2,1)} %wt_in.1, bf16[64,3072]{1,0:T(8,128)(2,1)} %pre_in.1, bf16[64,3072]{1,0:T(8,128)(2,1)} %og_in.1), custom_call_target="tpu_custom_call" | custom-call | tf_op jit(solution)/shard_map/exchange/pallas_call | solution.py:382
  82.6 6.6 %finish.1 = (bf16[384,3072]{1,0:T(8,128)(2,1)}, bf16[384,3072]{1,0:T(8,128)(2,1)}, bf16[384,3072]{1,0:T(8,128)(2,1)}, bf16[256,384]{1,0:T(8,128)(2,1)}) custom-call(bf16[3,384,2304]{2,1,0:T(8,128)(2,1)} %get-tuple-element.11.done_in, f32[384,768]{1,0:T(8,128)} %get-tuple-element.12.rest_in, bf16[256,384]{1,0:T(8,128)(2,1)} %get-tuple-element.13.dx_in), custom_call_target="tpu_custom_call" | custom-call | tf_op jit(solution)/shard_map/finish/pallas_call | solution.py:405

commit v3 on v2

--- a/solution.py
+++ b/solution.py
@@ -11,7 +11,7 @@
 MESH = pl.DeviceIdType.MESH
 BF, F32 = jnp.bfloat16, jnp.float32
 BLOCK = 384
-LATE = 2
+LATE = 1
 NT = (((1,), (1,)), ((), ()))
 NN = (((1,), (0,)), ((), ()))
 DIST = (0, 1, 7, 2, 6, 3, 5, 4)

time: 89.5 us -> 89.5 us (level)
  no operation moved by 1% of the time
where the time goes in v3:
time: 89.5 us; the launch traced here: 89.4 us
  Pallas kernels  88.6 us (99%)
    pallas_call x1, Pallas kernels, on_device(): pl.pallas_call(functools.partial(kernel, scale, early), out_shape=(jax.Sh...  82 us
    pallas_call x1, Pallas kernels, on_device(): pl.pallas_call(functools.partial(finish, scale, early), out_shape=(full,...  6.61 us

profile of v3, /device:TPU:2, one launch (start us, length us, event | category | flops | bytes accessed | tf_op | source)
XLA Modules:
  0.0 89.4 jit_solution(14717679612852373584)
XLA Ops:
  0.6 82.0 %exchange.1 = (bf16[3,384,2688]{2,1,0:T(8,128)(2,1)}, f32[384,384]{1,0:T(8,128)}, bf16[256,384]{1,0:T(8,128)(2,1)}) custom-call(bf16[256,384]{1,0:T(8,128)(2,1)} %tok_in.1, bf16[384,3072]{1,0:T(8,128)(2,1)} %wt_in.1, bf16[64,3072]{1,0:T(8,128)(2,1)} %pre_in.1, bf16[64,3072]{1,0:T(8,128)(2,1)} %og_in.1), custom_call_target="tpu_custom_call" | custom-call | tf_op jit(solution)/shard_map/exchange/pallas_call | solution.py:382
  82.6 6.6 %finish.1 = (bf16[384,3072]{1,0:T(8,128)(2,1)}, bf16[384,3072]{1,0:T(8,128)(2,1)}, bf16[384,3072]{1,0:T(8,128)(2,1)}, bf16[256,384]{1,0:T(8,128)(2,1)}) custom-call(bf16[3,384,2688]{2,1,0:T(8,128)(2,1)} %get-tuple-element.11.done_in, f32[384,384]{1,0:T(8,128)} %get-tuple-element.12.rest_in, bf16[256,384]{1,0:T(8,128)(2,1)} %get-tuple-element.13.dx_in), custom_call_target="tpu_custom_call" | custom-call | tf_op jit(solution)/shard_map/finish/pallas_call | solution.py:405
